TPU v7x, 32 devices: a whole 2x2x4 slice. The times are simulated.
32 devices in a mesh: groups: 2 (over y), tensor: 4 (over z), dp: 4 (over x, core).
Axes of the slice: x: 2, y: 2, z: 4, core: 2. Of those that a mesh axis runs over, the one named last changes fastest.
Arguments:
- out_grad: bfloat16 [4, 1280, 4096], P('dp', ('groups', 'tensor')), parts along dimension 1, may hold values from -6 to 6
- gate_pre: bfloat16 [4, 1280, 14336], P('dp', 'groups', 'tensor'), parts along dimension 1, may hold values from -8 to 8
- up_pre: bfloat16 [4, 1280, 14336], P('dp', 'groups', 'tensor'), parts along dimension 1, may hold values from -6 to 6
- down_weight: bfloat16 [14336, 4096], P('tensor'), may hold values from -0.046875 to 0.046875
Outputs:
- gate_grad: bfloat16 [4, 1280, 14336], P('dp', 'groups', 'tensor'), parts along dimension 1
- up_grad: bfloat16 [4, 1280, 14336], P('dp', 'groups', 'tensor'), parts along dimension 1
- down_grad: bfloat16 [28672, 4096], P(('groups', 'tensor'), 'dp'), parts along dimension 0
There are 2 independent parts, one for each index of `groups`. A program takes and returns all parts, laid end to end along the dimension named above; an argument that names none is the same for every part. Nothing has to cross between parts.
All inputs are finite; a program needn't handle non-finite values.
Results may differ from a plain program's by a relative error of at most 0.014.
Values may be sent and summed in bfloat16 or wider, within the bound.
A program may use at most 128 MiB of HBM per device.

v0:
```python
import math
import jax
import jax.numpy as jnp
from jax import lax
from jax.sharding import PartitionSpec as P


def times_down(block, down_weight):
    return lax.dot_general(
        block, down_weight, (((1,), (1,)), ((), ())), preferred_element_type=jnp.float32
    )


def on_device(out_grad, gate_pre, up_pre, down_weight):
    gate = gate_pre[0].astype(jnp.float32)
    up = up_pre[0].astype(jnp.float32)
    sig = jax.nn.sigmoid(gate)
    act = gate * sig
    hidden = (act * up).astype(jnp.bfloat16)
    group_rows = hidden.shape[0]
    scale = 1.0 / math.sqrt(group_rows * lax.axis_size("dp"))
    block = lax.all_gather(out_grad, "tensor", axis=1, tiled=True)[0]
    weight_acc = jnp.einsum("tf,td->fd", hidden, block, preferred_element_type=jnp.float32)
    hidden_grad = times_down(block, down_weight)
    weight_acc, hidden_grad = (weight_acc, hidden_grad)
    down_grad = lax.psum_scatter(
        (weight_acc * scale).astype(jnp.bfloat16), "dp", scatter_dimension=1, tiled=True
    )
    gate_grad = (hidden_grad * up * sig * (1.0 + gate * (1.0 - sig))).astype(jnp.bfloat16)
    up_grad = (hidden_grad * act).astype(jnp.bfloat16)
    return (gate_grad[None], up_grad[None], down_grad)


def solution(mesh):
    return jax.shard_map(
        on_device,
        mesh=mesh,
        in_specs=(
            P("dp", ("groups", "tensor"), None),
            P("dp", "groups", "tensor"),
            P("dp", "groups", "tensor"),
            P("tensor", None),
        ),
        out_specs=(
            P("dp", "groups", "tensor"),
            P("dp", "groups", "tensor"),
            P(("groups", "tensor"), "dp"),
        ),
        check_vma=False,
    )
```

profile of v0, /device:TPU:0, one launch (start us, length us, event | category | flops | bytes accessed | tf_op | source)
XLA Modules:
  0.0 359.5 jit_solution(4585248660754477539)
XLA Ops:
  7.2 0.0 all-gather.2.cloned.1.call-start
  7.2 0.7 all-gather.2.cloned.1.call-update
  7.9 0.0 reduce-scatter.2.cloned.1.call-start
  7.9 102.4 %all-gather.2.cloned.1.call-done = bf16[1,640,4096]{2,1,0:T(8,128)(2,1)} async-done(((bf16[1,160,4096]{2,1,0:T(8,128)(2,1)}), bf16[1,640,4096]{2,1,0:T(8,128)(2,1)}) %all-gather.2.cloned.1.call-update) | async-done | bytes 5242896 | tf_op jit(solution)/shard_map/all_gather | solution.py:22
  110.4 35.9 %multiply_convert_fusion = bf16[3584,4096]{1,0:T(8,128)(2,1)} fusion(bf16[1,640,4096]{2,1,0:T(8,128)(2,1)} %all-gather.2.cloned.1.call-done, bf16[1,640,3584]{2,1,0:T(8,128)(2,1)} %param.6, bf16[1,640,3584]{2,1,0:T(8,128)(2,1)} %param.5), kind=kOutput, calls=%fused_computation | convolution fusion | flops 18838192128 | bytes 43778048 | tf_op jit(solution)/shard_map/tf,td->fd/dot_general | solution.py:23
  146.3 0.0 reduce-scatter.2.cloned.1.call-update
  146.3 34.0 %fusion.22 = (bf16[1,640,3584]{2,1,0:T(8,128)(2,1)}, bf16[1,640,3584]{2,1,0:T(8,128)(2,1)}) fusion(bf16[1,640,3584]{2,1,0:T(8,128)(2,1)} %param.5, bf16[1,640,3584]{2,1,0:T(8,128)(2,1)} %param.6, bf16[3584,4096]{1,0:T(8,128)(2,1)} %param.7, bf16[1,640,4096]{2,1,0:T(8,128)(2,1)} %all-gather.2.cloned.1.call-done), kind=kOutput, calls=%fused_computation.27 | convolution fusion | flops 18824888320 | bytes 52953088 | tf_op jit(solution)/shard_map/dot_general | solution.py:9
  180.3 172.4 %reduce-scatter.2.cloned.1.call-done = bf16[3584,1024]{1,0:T(8,128)(2,1)} async-done(((bf16[3584,4096]{1,0:T(8,128)(2,1)}), bf16[3584,1024]{1,0:T(8,128)(2,1)}) %reduce-scatter.2.cloned.1.call-update) | async-done | bytes 7340048 | tf_op jit(solution)/shard_map/reduce_scatter | solution.py:26
Async XLA Ops:
  7.2 103.2 %all-gather.2.cloned.1.call-start = ((), (), s32[]{:S(2)}) async-start(), calls=%async_computation.1 | async-start | bytes 6553600 | tf_op jit(solution)/shard_map/all_gather | solution.py:22
  7.9 344.8 %reduce-scatter.2.cloned.1.call-start = ((), (), s32[]{:S(2)}) async-start(), calls=%async_computation.2 | async-start | bytes 36700160 | tf_op jit(solution)/shard_map/reduce_scatter | solution.py:26
Sparse Core Ops, SparseCore 0:
  9.6 100.7 all-gather.1
  146.4 206.2 reduce-scatter.1
where the time goes:
time: 360 us
  waiting for transfers between devices  275 us (76%)
  matrix products  69.9 us (19%)
  between operations  14 us (4%)
    reduce_scatter x1, waiting for transfers between devices, on_device(): lax.psum_scatter((weight_acc * scale).astype(jnp.bfloat16), 'dp', scatter...  172 us
    all_gather x1, waiting for transfers between devices, on_device(): block = lax.all_gather(out_grad, 'tensor', axis=1, tiled=True)[0]  102 us
    dot_general x1, matrix products, on_device(): jnp.einsum('tf,td->fd', hidden, block, preferred_element_type=jnp.float32)  35.9 us
    dot_general x1, matrix products, times_down(): lax.dot_general(block, down_weight, (((1,), (1,)), ((), ())), preferred_e...  34 us
  transfers between devices with their start and end apart: 2, of which 2 were waited for; matrix products, arithmetic and copies ran while one was open for 9% of the time, Pallas kernels for 0%

commit v1 on v0

--- a/solution.py
+++ b/solution.py
@@ -1,8 +1,40 @@
+import functools
 import math
 import jax
 import jax.numpy as jnp
 from jax import lax
 from jax.sharding import PartitionSpec as P
+
+
+def post_sources_all(incoming_x, link_axis, d0):
+    far_arr, local_out, h_now = (
+        lax.axis_size(link_axis),
+        lax.axis_index(link_axis),
+        incoming_x.shape[d0],
+    )
+    buffers = [j * far_arr if it == d0 else j for it, j in enumerate(incoming_x.shape)]
+    n_now = lax.dynamic_update_slice_in_dim(
+        jnp.zeros(buffers, incoming_x.dtype), incoming_x, local_out * h_now, axis=d0
+    )
+    mat_out = z2 = incoming_x
+    for ii in [*range(1, far_arr // 2 + 1)]:
+        mat_out = lax.ppermute(
+            mat_out, axis_name=link_axis, perm=[(it, (it + 1) % far_arr) for it in range(far_arr)]
+        )
+        n_now = lax.dynamic_update_slice_in_dim(
+            n_now, mat_out, (local_out - ii) % far_arr * h_now, axis=d0
+        )
+        if 2 * ii < far_arr:
+            z2 = lax.ppermute(
+                z2, axis_name=link_axis, perm=[(it, (it - 1) % far_arr) for it in range(far_arr)]
+            )
+            n_now = lax.dynamic_update_slice_in_dim(
+                n_now, z2, (local_out + ii) % far_arr * h_now, axis=d0
+            )
+    return n_now
+
+
+wrap_stages_all_on = functools.partial(post_sources_all, link_axis="tensor", d0=1)
 
 
 def times_down(block, down_weight):
@@ -19,7 +51,7 @@
     hidden = (act * up).astype(jnp.bfloat16)
     group_rows = hidden.shape[0]
     scale = 1.0 / math.sqrt(group_rows * lax.axis_size("dp"))
-    block = lax.all_gather(out_grad, "tensor", axis=1, tiled=True)[0]
+    block = wrap_stages_all_on(out_grad)[0]
     weight_acc = jnp.einsum("tf,td->fd", hidden, block, preferred_element_type=jnp.float32)
     hidden_grad = times_down(block, down_weight)
     weight_acc, hidden_grad = (weight_acc, hidden_grad)

time: 360 us -> 343 us (0.953)
  waiting for transfers between devices: 275 us -> 251 us
  local copies, waits for them, and re-layouts: 0 us -> 9.05 us
  matrix products: 69.9 us -> 63.8 us
  starting transfers between devices: 0.08 us -> 5.21 us
    all_gather x1 -> x0, waiting for transfers between devices: 102 us -> none  [on_device(): block = lax.all_gather(out_grad, 'tensor', axis=1, tiled=True)[0]]
    ppermute x0 -> x3, waiting for transfers between devices: none -> 77.3 us  [the longest x2 51.5 us: post_sources_all(): lax.ppermute(mat_out, axis_name=link_axis, perm=[(it, (it + 1) % far_arr)...]
    dynamic_update_slice x0 -> x4, local copies, waits for them, and re-layouts: none -> 6.1 us  [the longest x1 2.51 us: post_sources_all(): lax.dynamic_update_slice_in_dim(n_now, z2, (local_out + ii) % far_arr * h...]
    dot_general x1, matrix products: 35.9 us -> 30.2 us  [on_device(): jnp.einsum('tf,td->fd', hidden, block, preferred_element_type=jnp.float32)]
    ppermute x0 -> x3, starting transfers between devices: none -> 5.17 us  [the longest x2 3.08 us: post_sources_all(): lax.ppermute(mat_out, axis_name=link_axis, perm=[(it, (it + 1) % far_arr)...]
  transfers between devices with their start and end apart: 2 -> 4, of which waited for: 2 -> 4; matrix products, arithmetic and copies ran while one was open for 9% -> 12% of each run, Pallas kernels for 0% -> 0%
where the time goes in v1:
time: 343 us
  waiting for transfers between devices  251 us (73%)
  matrix products  63.8 us (19%)
  between operations  14 us (4%)
  local copies, waits for them, and re-layouts  9.05 us (3%)
  starting transfers between devices  5.21 us (2%)
    reduce_scatter x1, waiting for transfers between devices, on_device(): lax.psum_scatter((weight_acc * scale).astype(jnp.bfloat16), 'dp', scatter...  174 us
    ppermute x2, waiting for transfers between devices, post_sources_all(): lax.ppermute(mat_out, axis_name=link_axis, perm=[(it, (it + 1) % far_arr)...  51.5 us
    dot_general x1, matrix products, times_down(): lax.dot_general(block, down_weight, (((1,), (1,)), ((), ())), preferred_e...  33.6 us
    dot_general x1, matrix products, on_device(): jnp.einsum('tf,td->fd', hidden, block, preferred_element_type=jnp.float32)  30.2 us
    ppermute x1, waiting for transfers between devices, post_sources_all(): lax.ppermute(z2, axis_name=link_axis, perm=[(it, (it - 1) % far_arr) for...  25.8 us
  transfers between devices with their start and end apart: 4, of which 4 were waited for; matrix products, arithmetic and copies ran while one was open for 12% of the time, Pallas kernels for 0%

profile of v1, /device:TPU:0, one launch (start us, length us, event | category | flops | bytes accessed | tf_op | source)
XLA Modules:
  0.0 343.1 jit_solution(6140604258876563218)
XLA Ops:
  7.2 0.0 copy-start
  7.2 0.0 reduce-scatter.2.cloned.1.call-start
  7.2 3.1 collective-permute-start
  10.3 2.1 collective-permute-start.1
  12.4 2.9 squeeze.13
  15.3 0.0 copy-done
  15.3 0.0 slice-start
  15.3 1.2 bitcast_dynamic-update-slice_fusion.3
  16.5 0.0 slice-start.1
  16.5 25.6 %collective-permute-done = bf16[1,160,4096]{2,1,0:T(8,128)(2,1)S(1)} collective-permute-done((bf16[1,160,4096]{2,1,0:T(8,128)(2,1)}, bf16[1,160,4096]{2,1,0:T(8,128)(2,1)S(1)}, u32[]{:S(2)}, u32[]{:S(2)}) %collective-permute-start) | collective-permute-done | bytes 1310752 | tf_op jit(solution)/shard_map/ppermute | solution.py:21
  42.2 0.0 collective-permute-start.2
  42.2 1.2 bitcast_dynamic-update-slice_fusion.2
  43.4 25.8 %collective-permute-done.1 = bf16[1,160,4096]{2,1,0:T(8,128)(2,1)} collective-permute-done((bf16[1,160,4096]{2,1,0:T(8,128)(2,1)}, bf16[1,160,4096]{2,1,0:T(8,128)(2,1)}, u32[]{:S(2)}, u32[]{:S(2)}) %collective-permute-start.1) | collective-permute-done | bytes 1310752 | tf_op jit(solution)/shard_map/ppermute | solution.py:28
  69.2 2.5 bitcast_dynamic-update-slice_fusion.1
  71.7 25.9 %collective-permute-done.2 = bf16[1,160,4096]{2,1,0:T(8,128)(2,1)S(1)} collective-permute-done((bf16[1,160,4096]{2,1,0:T(8,128)(2,1)S(1)}, bf16[1,160,4096]{2,1,0:T(8,128)(2,1)S(1)}, u32[]{:S(2)}, u32[]{:S(2)}) %collective-permute-start.2) | collective-permute-done | bytes 1310752 | tf_op jit(solution)/shard_map/ppermute | solution.py:21
  97.5 1.2 bitcast_dynamic-update-slice_fusion
  98.7 0.0 slice-done
  98.7 0.0 slice-done.1
  98.7 30.2 %multiply_convert_fusion = bf16[3584,4096]{1,0:T(8,128)(2,1)} fusion(bf16[640,4096]{1,0:T(8,128)(2,1)} %bitcast_dynamic-update-slice_fusion, bf16[1,640,3584]{2,1,0:T(8,128)(2,1)} %param.6, bf16[1,640,3584]{2,1,0:T(8,128)(2,1)S(1)} %bitcast.36), kind=kOutput, calls=%fused_computation | convolution fusion | flops 18838192128 | bytes 43778048 | tf_op jit(solution)/shard_map/tf,td->fd/dot_general | solution.py:55
  128.9 0.0 reduce-scatter.2.cloned.1.call-update
  128.9 33.6 %fusion.8 = (bf16[1,640,3584]{2,1,0:T(8,128)(2,1)}, bf16[1,640,3584]{2,1,0:T(8,128)(2,1)}) fusion(bf16[1,640,3584]{2,1,0:T(8,128)(2,1)} %param.5, bf16[1,640,3584]{2,1,0:T(8,128)(2,1)} %param.6, bf16[640,4096]{1,0:T(8,128)(2,1)} %bitcast_dynamic-update-slice_fusion, bf16[3584,4096]{1,0:T(8,128)(2,1)} %param.7), kind=kOutput, calls=%fused_computation.15 | convolution fusion | flops 18824888320 | bytes 52953088 | tf_op jit(solution)/shard_map/dot_general | solution.py:41
  162.5 173.8 %reduce-scatter.2.cloned.1.call-done = bf16[3584,1024]{1,0:T(8,128)(2,1)} async-done(((bf16[3584,4096]{1,0:T(8,128)(2,1)}), bf16[3584,1024]{1,0:T(8,128)(2,1)}) %reduce-scatter.2.cloned.1.call-update) | async-done | bytes 7340048 | tf_op jit(solution)/shard_map/reduce_scatter | solution.py:58
  (1 shorter events, 0.0 us)
Async XLA Ops:
  7.2 8.2 %copy-start = (bf16[1,160,4096]{2,1,0:T(8,128)(2,1)S(1)}, bf16[1,160,4096]{2,1,0:T(8,128)(2,1)}, u32[]{:S(2)}) copy-start(bf16[1,160,4096]{2,1,0:T(8,128)(2,1)} %param.4) | copy-start | bytes 3932164
  7.2 329.1 %reduce-scatter.2.cloned.1.call-start = ((), (), s32[]{:S(2)}) async-start(), calls=%async_computation.1 | async-start | bytes 36700160 | tf_op jit(solution)/shard_map/reduce_scatter | solution.py:58
  7.2 35.0 %collective-permute-start = (bf16[1,160,4096]{2,1,0:T(8,128)(2,1)}, bf16[1,160,4096]{2,1,0:T(8,128)(2,1)S(1)}, u32[]{:S(2)}, u32[]{:S(2)}) collective-permute-start(bf16[1,160,4096]{2,1,0:T(8,128)(2,1)} %param.4), channel_id=1, source_target_pairs={{0,4},{4,8},{8,12},{12,0},{1,5},{5,9},{9,13},{13,1},{2,6},{6,10},{... | collective-permute-start | bytes 3932168 | tf_op jit(solution)/shard_map/ppermute | solution.py:21
  10.3 58.9 %collective-permute-start.1 = (bf16[1,160,4096]{2,1,0:T(8,128)(2,1)}, bf16[1,160,4096]{2,1,0:T(8,128)(2,1)}, u32[]{:S(2)}, u32[]{:S(2)}) collective-permute-start(bf16[1,160,4096]{2,1,0:T(8,128)(2,1)} %param.4), channel_id=1, source_target_pairs={{0,12},{4,0},{8,4},{12,8},{1,13},{5,1},{9,5},{13,9},{2,14},{6,2},{... | collective-permute-start | bytes 3932168 | tf_op jit(solution)/shard_map/ppermute | solution.py:28
  15.3 83.4 %slice-start = ((s8[4587520]{0:T(1024)(128)(4,1)}), s8[393216]{0:T(1024)(128)(4,1)S(1)}, s32[]{:S(2)}) async-start(s8[4587520]{0:T(1024)(128)(4,1)} %bitcast.35), calls=%async_computation.2 | async-start | bytes 786432
  16.5 82.2 %slice-start.1 = ((s8[4587520]{0:T(1024)(128)(4,1)}), s8[4194304]{0:T(1024)(128)(4,1)S(1)}, s32[]{:S(2)}) async-start(s8[4587520]{0:T(1024)(128)(4,1)} %bitcast.35), calls=%async_computation.3 | async-start | bytes 8388608
  42.2 55.3 %collective-permute-start.2 = (bf16[1,160,4096]{2,1,0:T(8,128)(2,1)S(1)}, bf16[1,160,4096]{2,1,0:T(8,128)(2,1)S(1)}, u32[]{:S(2)}, u32[]{:S(2)}) collective-permute-start(bf16[1,160,4096]{2,1,0:T(8,128)(2,1)S(1)} %collective-permute-done), channel_id=1, source_target_pairs={{0,4},{4,8},{8,12},{12,0},{1,5},{5,9},{9,13},{13,1},{2,6},{6,10},{... | collective-permute-start | bytes 3932168 | tf_op jit(solution)/shard_map/ppermute | solution.py:21
Sparse Core Ops, SparseCore 0:
  129.1 207.1 reduce-scatter.1
